TPU v7x, 256 devices: a whole 4x4x8 slice. The times are simulated.
256 devices in a mesh: src: 128 (over x, z, y), lev: 2 (over core).
Axes of the slice: x: 4, y: 4, z: 8, core: 2. Of those that a mesh axis runs over, the one named last changes fastest.
Arguments:
- field: bfloat16 [262144, 256], P('src', 'lev'), may hold values from -6 to 6
- grad_coef: float32 [2, 4, 262144], P(None, None, 'src'), may hold values from -6 to 6
- neighbours: int32 [262144, 4], P('src'), may hold values from 0 to 2175, as said below
- level_weight: float32 [8], replicated, may hold values from 0.2 to 2
- src_index: int32 [16384, 64], P('src'), may hold values from 0 to 2047
- tgt_index: int32 [16384, 32], P('src'), may hold values from 0 to 1023
- block_dest: int32 [16384, 1], P('src'), may hold values from 0 to 127; in each aligned block of 128 rows (0 to 127, 128 to 255, ...) at most 2 rows name the same one
- weights: bfloat16 [16384, 6144], P('src'), may hold values from -0.21875 to 0.21875
Outputs:
- remapped: bfloat16 [131072, 256], P('src', 'lev')
- column_total: float32 [32, 131072], P(None, 'src')
Inputs may be any that keep to these rules, and one draw needn't show every extreme that they name: `neighbours`: position 64 + p is the device's own cell p; positions below 64 and from 2112 on are the last and first cells of the devices before and after along the closed curve; a neighbour lies at most 64 cells from the cell. `block_dest`: the 128 blocks of one index of src name one target index at most 2 times.
All inputs are finite; a program needn't handle non-finite values.
Results may differ from a plain program's by a relative error of at most 0.0049.
Values may be sent and summed in bfloat16 or wider, within the bound.
No kernel may reach another device: no remote copies, remote signals or barrier semaphores. Data moves between devices by JAX's collectives and lax.ppermute only.
A program may use at most 128 MiB of HBM per device.

v0:
```python
import jax
import jax.numpy as jnp
from jax import lax
from jax.sharding import PartitionSpec as P

FIELDS = 32
HW = 64
SB = 64
TB = 32
T_DEV = 1024


def extended_2(block, sides, width):
    for axis, dim in sides:
        count = lax.axis_size(axis)
        forward = [(i, i + 1) for i in range(count - 1)]
        forward.append((count - 1, 0))
        backward = [(target, source) for source, target in forward]
        low = lax.ppermute(
            lax.slice_in_dim(block, block.shape[dim] - width, None, axis=dim), axis, forward
        )
        high = lax.ppermute(lax.slice_in_dim(block, 0, width, axis=dim), axis, backward)
        block = jnp.concatenate([low, block, high], axis=dim)
    return block


def block_product(block_weights, block_rows):
    block_count = block_rows.shape[0]
    shaped = block_weights.reshape(block_count, 3 * SB, TB)
    return lax.dot_general(
        shaped, block_rows, (((1,), (1,)), ((0,), (0,))), preferred_element_type=jnp.float32
    )


def shards(field, grad_coef, neighbours, level_weight, src_index, tgt_index, block_dest, weights):
    extended = extended_2(field, (("src", 0),), HW)
    own_float = field.astype(jnp.float32)
    differ = extended[neighbours].astype(jnp.float32) - own_float[:, None, :]
    grad_east = jnp.sum(grad_coef[0].T[:, :, None] * differ, axis=1).astype(jnp.bfloat16)
    grad_north = jnp.sum(grad_coef[1].T[:, :, None] * differ, axis=1).astype(jnp.bfloat16)
    recon = jnp.stack([field, grad_east, grad_north])
    columns = field.shape[1]
    block_count = src_index.shape[0]
    block_rows = jnp.transpose(recon[:, src_index], (1, 0, 2, 3)).reshape(
        block_count, 3 * SB, columns
    )
    src_count = lax.axis_size("src")
    capacity = 2 * block_count // src_count
    target_owner = block_dest[:, 0]
    onehot = (target_owner[:, None] == jnp.arange(src_count, dtype=jnp.int32)[None, :]).astype(
        jnp.int32
    )
    before = jnp.cumsum(onehot, axis=0) - onehot
    slot_rank = jnp.sum(before * onehot, axis=1)
    slot_index = target_owner * capacity + slot_rank
    slots = src_count * capacity
    send_cells = jnp.zeros((slots, TB), jnp.int32).at[slot_index].set(tgt_index)
    recv_cells = lax.all_to_all(send_cells, "src", split_axis=0, concat_axis=0, tiled=True)
    send_rows = jnp.zeros((slots, 3 * SB, columns), jnp.bfloat16).at[slot_index].set(block_rows)
    send_weights = jnp.zeros((slots, weights.shape[1]), jnp.bfloat16).at[slot_index].set(weights)
    got_rows, got_weights = (
        lax.all_to_all(send_rows, "src", split_axis=0, concat_axis=0, tiled=True),
        lax.all_to_all(send_weights, "src", split_axis=0, concat_axis=0, tiled=True),
    )
    received = block_product(got_weights, got_rows)
    total = (
        jnp.zeros((T_DEV, columns), jnp.float32)
        .at[recv_cells.reshape(-1)]
        .add(received.reshape(-1, columns))
    )
    remapped = total.astype(jnp.bfloat16)
    level_count = columns // FIELDS
    level_share = lax.dynamic_slice_in_dim(
        level_weight, lax.axis_index("lev") * level_count, level_count
    )
    local_sum = jnp.einsum(
        "tlf,l->ft",
        total.reshape(T_DEV, level_count, FIELDS),
        level_share,
        precision=lax.Precision.HIGHEST,
    )
    column_total = lax.psum(local_sum, "lev")
    return (remapped, column_total)


def solution(mesh):
    placed = (
        P("src", "lev"),
        P(None, None, "src"),
        P("src", None),
        P(),
        P("src", None),
        P("src", None),
        P("src", None),
        P("src", None),
    )
    return jax.shard_map(
        shards,
        mesh=mesh,
        in_specs=placed,
        out_specs=(P("src", "lev"), P(None, "src")),
        check_vma=False,
    )
```

profile of v0, /device:TPU:1, one launch (start us, length us, event | category | flops | bytes accessed | tf_op | source)
XLA Modules:
  0.0 694.0 jit_solution(10365732698928579888)
XLA Ops:
  7.2 0.0 copy-start
  7.2 0.7 fusion.10
  7.9 0.2 reduce_window_sum.11
  8.1 0.8 select_reduce_fusion
  8.9 0.7 fusion.13
  9.6 0.8 copy.21
  10.4 1.5 scatter_custom_fusion
  11.9 16.3 %all-to-all-start = ((s32[128,2,32]{2,1,0:T(2,128)}), s32[128,2,32]{2,1,0:T(2,128)S(1)}, u32[]{:S(2)}, u32[]{:S(2)}) async-start(s32[128,2,32]{2,1,0:T(2,128)} %bitcast.3), calls=%async_computation | async-start | bytes 262144 | tf_op jit(solution)/shard_map/all_to_all | solution.py:58
  28.2 4.6 scatter_custom_fusion.1
  32.9 3.3 all_to_all.17
  36.2 0.0 copy-start.1
  36.2 0.0 copy-start.4
  36.2 0.0 copy-start.5
  36.2 0.0 copy-start.3
  36.2 3.0 all-to-all-done
  39.2 10.9 %all-to-all-start.1 = ((bf16[128,2,6144]{2,1,0:T(2,128)(2,1)}), bf16[128,2,6144]{2,1,0:T(2,128)(2,1)}, u32[]{:S(2)}, u32[]{:S(2)}) async-start(bf16[128,2,6144]{2,1,0:T(2,128)(2,1)} %all_to_all.17), calls=%async_computation.1 | async-start | bytes 6291456 | tf_op jit(solution)/shard_map/all_to_all | solution.py:63
  50.1 0.0 copy-done.1
  50.1 0.6 collective-permute-start
  50.7 6.8 collective-permute-start.1
  57.5 0.0 copy-done.4
  57.5 0.4 copy.23
  57.9 0.6 reshape.80
  58.6 0.0 copy-done.5
  58.6 0.1 copy.28
  58.7 0.1 reshape.88
  58.8 0.0 copy-done.3
  58.8 1.1 convert_element_type.40
  59.9 1.4 copy.22
  61.3 1.4 copy.24
  62.6 8.9 %copy.25 = bf16[1,2048,128]{2,0,1:T(2,128)(2,1)} copy(bf16[1,2048,128]{2,1,0:T(8,128)(2,1)S(1)} %bitcast.44) | data formatting | bytes 1048576 | tf_op jit(solution)/shard_map/stack | solution.py:41
  71.5 49.4 %collective-permute-done = bf16[64,128]{1,0:T(8,128)(2,1)S(1)} collective-permute-done((bf16[64,128]{1,0:T(8,128)(2,1)S(1)}, bf16[64,128]{1,0:T(8,128)(2,1)S(1)}, u32[]{:S(2)}, u32[]{:S(2)}) %collective-permute-start) | collective-permute-done | bytes 16416 | tf_op jit(solution)/shard_map/ppermute | solution.py:19
  121.0 0.0 collective-permute-done.1
  121.0 24.0 %gather_fusion = bf16[8192,128]{1,0:T(8,128)(2,1)S(1)} fusion(bf16[2176,128]{1,0:T(8,128)(2,1)S(1)} %pad_maximum_fusion.1, s32[8192]{0:T(1024)S(1)} %broadcast_clamp_fusion.1), kind=kCustom, calls=%fused_computation | custom fusion | bytes 4227072 | tf_op jit(solution)/shard_map/gather | solution.py:38
  145.1 0.0 copy-start.2
  145.1 15.1 %fusion.2 = (bf16[2048,128]{1,0:T(8,128)(2,1)S(1)}, bf16[2048,128]{1,0:T(8,128)(2,1)S(1)}) fusion(bf16[2048,4,128]{2,1,0:T(4,128)(2,1)S(1)} %bitcast.43, f32[2048,128]{1,0:T(8,128)} %convert_element_type.40, f32[2048,4]{1,0:T(8,128)} %copy.22, f32[2048,4]{1,0:T(8,128)} %copy.24), kind=kLoop, calls=%fused_computation.9 | loop fusion | flops 5767168 | bytes 4259840 | tf_op jit(solution)/shard_map/reduce_sum | solution.py:39
  160.1 8.1 %copy.26 = bf16[1,2048,128]{2,0,1:T(2,128)(2,1)S(1)} copy(bf16[1,2048,128]{2,1,0:T(8,128)(2,1)S(1)} %bitcast.47) | data formatting | bytes 1048576 | tf_op jit(solution)/shard_map/convert_element_type | solution.py:39
  168.3 8.3 %copy.27 = bf16[1,2048,128]{2,0,1:T(2,128)(2,1)S(1)} copy(bf16[1,2048,128]{2,1,0:T(8,128)(2,1)S(1)} %bitcast.46) | data formatting | bytes 1048576 | tf_op jit(solution)/shard_map/convert_element_type | solution.py:40
  176.6 0.0 copy-done.2
  176.6 3.6 pad_maximum_fusion
  180.2 56.5 %gather_fusion.1 = bf16[8192,3,128]{2,1,0:T(4,128)(2,1)} fusion(bf16[3,2048,128]{2,0,1:T(4,128)(2,1)S(1)} %pad_maximum_fusion, s32[8192]{0:T(1024)S(1)} %broadcast_clamp_fusion), kind=kCustom, calls=%fused_computation.1 | custom fusion | bytes 12615680 | tf_op jit(solution)/shard_map/gather | solution.py:44
  236.6 8.0 %copy.29 = bf16[128,64,3,128]{3,1,2,0:T(8,128)(2,1)} copy(bf16[128,64,3,128]{3,2,1,0:T(4,128)(2,1)} %bitcast.40) | data formatting | bytes 12582912 | tf_op jit(solution)/shard_map/gather | solution.py:44
  244.7 7.8 %broadcast_in_dim.29 = bf16[256,192,128]{2,1,0:T(8,128)(2,1)} broadcast(bf16[]{:T(256)} %constant.16.clone.1), dimensions={} | broadcast | bytes 12582914 | tf_op jit(solution)/shard_map/broadcast_in_dim | solution.py:59
  252.4 21.5 %scatter_fusion = bf16[256,192,128]{2,1,0:T(8,128)(2,1)} fusion(bf16[256,192,128]{2,1,0:T(8,128)(2,1)} %broadcast_in_dim.29, s32[128]{0:T(128)S(1)} %fusion.13, bf16[128,192,128]{2,1,0:T(8,128)(2,1)} %bitcast.41), kind=kCustom, calls=%fused_computation.4 | custom fusion | bytes 18874880 | tf_op jit(solution)/shard_map/scatter | solution.py:59
  274.0 0.0 all-to-all-done.1
  274.0 9.4 %all-to-all-start.2 = ((bf16[256,192,128]{2,1,0:T(8,128)(2,1)}), bf16[256,192,128]{2,1,0:T(8,128)(2,1)}, u32[]{:S(2)}, u32[]{:S(2)}) async-start(bf16[256,192,128]{2,1,0:T(8,128)(2,1)} %scatter_fusion), calls=%async_computation.2 | async-start | bytes 25165824 | tf_op jit(solution)/shard_map/all_to_all | solution.py:62
  283.3 0.0 all-reduce.2.cloned.1.call-start
  283.4 0.2 reshape.73
  283.6 16.2 %reshape.74 = bf16[256,192,32]{2,1,0:T(8,128)(2,1)} reshape(bf16[128,2,6144]{2,1,0:T(2,128)(2,1)} %all-to-all-done.1) | data formatting | bytes 6291456 | tf_op jit(solution)/shard_map/reshape | solution.py:29
  299.8 254.6 %all-to-all-done.2 = bf16[256,192,128]{2,1,0:T(8,128)(2,1)} async-done(((bf16[256,192,128]{2,1,0:T(8,128)(2,1)}), bf16[256,192,128]{2,1,0:T(8,128)(2,1)}, u32[]{:S(2)}, u32[]{:S(2)}) %all-to-all-start.2) | async-done | bytes 12582944 | tf_op jit(solution)/shard_map/all_to_all | solution.py:62
  554.4 12.1 %fusion.17 = f32[256,32,128]{2,1,0:T(8,128)} fusion(bf16[256,192,32]{2,1,0:T(8,128)(2,1)} %reshape.74, bf16[256,192,128]{2,1,0:T(8,128)(2,1)} %all-to-all-done.2), kind=kOutput, calls=%fused_computation.39 | convolution fusion | flops 402653184 | bytes 19922944 | tf_op jit(solution)/shard_map/dot_general | solution.py:30
  566.4 44.4 %scatter_custom_fusion.3 = f32[1024,128]{1,0:T(8,128)S(1)} fusion(s32[8192]{0:T(1024)S(1)} %bitcast.49, f32[8192,128]{1,0:T(8,128)} %bitcast.42, f32[]{:T(128)} %constant.11.clone.1), kind=kCustom, calls=%fused_computation.19 | custom fusion | flops 1048576 | bytes 524800 | tf_op jit(solution)/shard_map/scatter-add | solution.py:69
  610.9 0.2 copy.31
  611.1 0.0 copy-done
  611.1 28.9 %fusion.6 = f32[1,1024,32]{0,1,2:T(8,128)} fusion(f32[1024,4,32]{0,2,1:T(8,128)S(1)} %bitcast.45, f32[8]{0:T(128)S(1)} %copy-done, s32[]{:T(128)S(6)} %select_n.29), kind=kOutput, calls=%fused_computation.15 | convolution fusion | flops 1572864 | bytes 655396 | tf_op jit(solution)/shard_map/tlf,l->ft/dot_general | solution.py:76
  640.0 10.6 %copy.34 = f32[1,1024,32]{1,2,0:T(8,128)} copy(f32[1,1024,32]{0,1,2:T(8,128)} %fusion.6) | data formatting | bytes 262144 | tf_op jit(solution)/shard_map/tlf,l->ft/dot_general | solution.py:76
  650.5 0.0 all-reduce.2.cloned.1.call-update
  650.6 0.7 convert_element_type.45
  651.3 34.0 %all-reduce.2.cloned.1.call-done = f32[32,1024]{1,0:T(8,128)} async-done(((f32[32,1024]{1,0:T(8,128)}), f32[32,1024]{1,0:T(8,128)}) %all-reduce.2.cloned.1.call-update) | async-done | bytes 131088 | tf_op jit(solution)/shard_map/psum | solution.py:82
  685.3 1.6 copy.39
  (8 shorter events, 0.1 us)
Async XLA Ops:
  7.2 603.9 %copy-start = (f32[8]{0:T(128)S(1)}, f32[8]{0:T(128)}, u32[]{:S(2)}) copy-start(f32[8]{0:T(128)} %param.11) | copy-start | bytes 100
  11.9 27.3 %all-to-all-start = ((s32[128,2,32]{2,1,0:T(2,128)}), s32[128,2,32]{2,1,0:T(2,128)S(1)}, u32[]{:S(2)}, u32[]{:S(2)}) async-start(s32[128,2,32]{2,1,0:T(2,128)} %bitcast.3), calls=%async_computation | async-start | bytes 262144 | tf_op jit(solution)/shard_map/all_to_all | solution.py:58
  36.2 13.9 %copy-start.1 = (bf16[2048,128]{1,0:T(8,128)(2,1)S(1)}, bf16[2048,128]{1,0:T(8,128)(2,1)}, u32[]{:S(2)}) copy-start(bf16[2048,128]{1,0:T(8,128)(2,1)} %param.8) | copy-start | bytes 1572868
  36.2 21.3 %copy-start.4 = (s32[2048,4]{0,1:T(4,128)S(1)}, s32[2048,4]{0,1:T(4,128)}, u32[]{:S(2)}) copy-start(s32[2048,4]{0,1:T(4,128)} %param.10) | copy-start | bytes 98308
  36.2 22.3 %copy-start.5 = (s32[128,64]{0,1:T(8,128)S(1)}, s32[128,64]{0,1:T(8,128)}, u32[]{:S(2)}) copy-start(s32[128,64]{0,1:T(8,128)} %param.12) | copy-start | bytes 98308
  36.2 22.5 %copy-start.3 = (f32[2,4,2048]{2,1,0:T(4,128)S(1)}, f32[2,4,2048]{2,1,0:T(4,128)}, u32[]{:S(2)}) copy-start(f32[2,4,2048]{2,1,0:T(4,128)} %param.9) | copy-start | bytes 196612
  39.2 234.8 %all-to-all-start.1 = ((bf16[128,2,6144]{2,1,0:T(2,128)(2,1)}), bf16[128,2,6144]{2,1,0:T(2,128)(2,1)}, u32[]{:S(2)}, u32[]{:S(2)}) async-start(bf16[128,2,6144]{2,1,0:T(2,128)(2,1)} %all_to_all.17), calls=%async_computation.1 | async-start | bytes 6291456 | tf_op jit(solution)/shard_map/all_to_all | solution.py:63
  50.1 70.9 %collective-permute-start = (bf16[64,128]{1,0:T(8,128)(2,1)S(1)}, bf16[64,128]{1,0:T(8,128)(2,1)S(1)}, u32[]{:S(2)}, u32[]{:S(2)}) collective-permute-start(bf16[64,128]{1,0:T(8,128)(2,1)S(1)} %get-tuple-element.4), channel_id=1, source_target_pairs={{0,2},{2,4},{4,6},{6,8},{8,10},{10,12},{12,14},{14,16},{16,18},{18... | collective-permute-start | bytes 49160 | tf_op jit(solution)/shard_map/ppermute | solution.py:19
  50.7 70.3 %collective-permute-start.1 = (bf16[64,128]{1,0:T(8,128)(2,1)S(1)}, bf16[64,128]{1,0:T(8,128)(2,1)S(1)}, u32[]{:S(2)}, u32[]{:S(2)}) collective-permute-start(bf16[64,128]{1,0:T(8,128)(2,1)S(1)} %get-tuple-element.5), channel_id=1, source_target_pairs={{2,0},{4,2},{6,4},{8,6},{10,8},{12,10},{14,12},{16,14},{18,16},{20... | collective-permute-start | bytes 49160 | tf_op jit(solution)/shard_map/ppermute | solution.py:22
  145.1 31.5 %copy-start.2 = (bf16[1,2048,128]{2,0,1:T(2,128)(2,1)S(1)}, bf16[1,2048,128]{2,0,1:T(2,128)(2,1)}, u32[]{:S(2)}) copy-start(bf16[1,2048,128]{2,0,1:T(2,128)(2,1)} %copy.25) | copy-start | bytes 1572868
  274.0 280.4 %all-to-all-start.2 = ((bf16[256,192,128]{2,1,0:T(8,128)(2,1)}), bf16[256,192,128]{2,1,0:T(8,128)(2,1)}, u32[]{:S(2)}, u32[]{:S(2)}) async-start(bf16[256,192,128]{2,1,0:T(8,128)(2,1)} %scatter_fusion), calls=%async_computation.2 | async-start | bytes 25165824 | tf_op jit(solution)/shard_map/all_to_all | solution.py:62
  283.3 402.0 %all-reduce.2.cloned.1.call-start = ((), (), s32[]{:S(2)}) async-start(), calls=%async_computation.3 | async-start | bytes 262144 | tf_op jit(solution)/shard_map/psum | solution.py:82
Sparse Core Ops, SparseCore 0:
  650.7 34.5 all-reduce.1
where the time goes:
time: 702 us; the launch traced here: 694 us
  waiting for transfers between devices  341 us (49%)
  local copies, waits for them, and re-layouts  186 us (26%)
  other arithmetic  67.4 us (10%)
  starting transfers between devices  44 us (6%)
  matrix products  40.9 us (6%)
  between operations  14.5 us (2%)
    all_to_all x1, waiting for transfers between devices, shards(): lax.all_to_all(send_rows, 'src', split_axis=0, concat_axis=0, tiled=True)  255 us
    gather x2, local copies, waits for them, and re-layouts, shards(): recon[:, src_index]  64.5 us
    ppermute x1, waiting for transfers between devices, extended_2(): lax.ppermute(lax.slice_in_dim(block, block.shape[dim] - width, None, axis...  49.4 us
    scatter-add x1, other arithmetic, shards(): total = jnp.zeros((T_DEV, columns), jnp.float32).at[recv_cells.reshape(-1...  44.4 us
    psum x1, waiting for transfers between devices, shards(): column_total = lax.psum(local_sum, 'lev')  34 us
    dot_general x1, matrix products, shards(): jnp.einsum('tlf,l->ft', total.reshape(T_DEV, level_count, FIELDS), level_...  28.9 us
    gather x1, local copies, waits for them, and re-layouts, shards(): differ = extended[neighbours].astype(jnp.float32) - own_float[:, None, :]  24 us
    scatter x1, local copies, waits for them, and re-layouts, shards(): jnp.zeros((slots, 3 * SB, columns), jnp.bfloat16).at[slot_index]  21.5 us
  transfers between devices with their start and end apart: 6, of which 4 were waited for; matrix products, arithmetic and copies ran while one was open for 27% of the time, Pallas kernels for 0%

commit v1 on v0

--- a/solution.py
+++ b/solution.py
@@ -79,7 +79,7 @@
         level_share,
         precision=lax.Precision.HIGHEST,
     )
-    column_total = lax.psum(local_sum, "lev")
+    column_total = jnp.sum(lax.all_gather(local_sum, "lev"), axis=0)
     return (remapped, column_total)
 
 

time: 702 us -> 665 us (0.947)
  waiting for transfers between devices: 341 us -> 308 us
  between operations: 14.5 us -> 1.09 us
  blocking collectives: 0 us -> 7.46 us
    psum x1 -> x0, waiting for transfers between devices: 34 us -> none  [shards(): column_total = lax.psum(local_sum, 'lev')]
    all_gather x0 -> x1, blocking collectives: none -> 7.46 us  [shards(): column_total = jnp.sum(lax.all_gather(local_sum, 'lev'), axis=0)]
  transfers between devices with their start and end apart: 6 -> 5, of which waited for: 4 -> 3; matrix products, arithmetic and copies ran while one was open for 27% -> 29% of each run, Pallas kernels for 0% -> 0%
where the time goes in v1:
time: 665 us; the launch traced here: 654 us
  waiting for transfers between devices  308 us (46%)
  local copies, waits for them, and re-layouts  184 us (28%)
  other arithmetic  68 us (10%)
  starting transfers between devices  44.2 us (7%)
  matrix products  40.9 us (6%)
  blocking collectives  7.46 us (1%)
    all_to_all x1, waiting for transfers between devices, shards(): lax.all_to_all(send_rows, 'src', split_axis=0, concat_axis=0, tiled=True)  256 us
    gather x2, local copies, waits for them, and re-layouts, shards(): recon[:, src_index]  64.5 us
    ppermute x1, waiting for transfers between devices, extended_2(): lax.ppermute(lax.slice_in_dim(block, block.shape[dim] - width, None, axis...  49.4 us
    scatter-add x1, other arithmetic, shards(): total = jnp.zeros((T_DEV, columns), jnp.float32).at[recv_cells.reshape(-1...  44.4 us
    dot_general x1, matrix products, shards(): jnp.einsum('tlf,l->ft', total.reshape(T_DEV, level_count, FIELDS), level_...  28.9 us
    gather x1, local copies, waits for them, and re-layouts, shards(): differ = extended[neighbours].astype(jnp.float32) - own_float[:, None, :]  24 us
    scatter x1, local copies, waits for them, and re-layouts, shards(): jnp.zeros((slots, 3 * SB, columns), jnp.bfloat16).at[slot_index]  21.5 us
    all_to_all x1, starting transfers between devices, shards(): lax.all_to_all(send_cells, 'src', split_axis=0, concat_axis=0, tiled=True)  16.3 us
  transfers between devices with their start and end apart: 5, of which 3 were waited for; matrix products, arithmetic and copies ran while one was open for 29% of the time, Pallas kernels for 0%

profile of v1, /device:TPU:1, one launch (start us, length us, event | category | flops | bytes accessed | tf_op | source)
XLA Modules:
  0.0 653.9 jit_solution(9968357007114933240)
XLA Ops:
  0.6 0.0 copy-start
  0.6 0.7 fusion.10
  1.4 0.2 reduce_window_sum.11
  1.6 0.8 select_reduce_fusion
  2.4 0.7 fusion.13
  3.1 0.8 copy.21
  3.9 1.5 scatter_custom_fusion
  5.4 16.3 %all-to-all-start = ((s32[128,2,32]{2,1,0:T(2,128)}), s32[128,2,32]{2,1,0:T(2,128)S(1)}, u32[]{:S(2)}, u32[]{:S(2)}) async-start(s32[128,2,32]{2,1,0:T(2,128)} %bitcast.3), calls=%async_computation | async-start | bytes 262144 | tf_op jit(solution)/shard_map/all_to_all | solution.py:58
  21.7 4.6 scatter_custom_fusion.1
  26.3 3.3 all_to_all.17
  29.7 0.0 copy-start.1
  29.7 0.0 copy-start.4
  29.7 0.0 copy-start.5
  29.7 0.0 copy-start.3
  29.7 3.0 all-to-all-done
  32.7 10.9 %all-to-all-start.1 = ((bf16[128,2,6144]{2,1,0:T(2,128)(2,1)}), bf16[128,2,6144]{2,1,0:T(2,128)(2,1)}, u32[]{:S(2)}, u32[]{:S(2)}) async-start(bf16[128,2,6144]{2,1,0:T(2,128)(2,1)} %all_to_all.17), calls=%async_computation.1 | async-start | bytes 6291456 | tf_op jit(solution)/shard_map/all_to_all | solution.py:63
  43.6 0.0 copy-done.1
  43.6 0.6 collective-permute-start
  44.2 6.8 %collective-permute-start.1 = (bf16[64,128]{1,0:T(8,128)(2,1)S(1)}, bf16[64,128]{1,0:T(8,128)(2,1)S(1)}, u32[]{:S(2)}, u32[]{:S(2)}) collective-permute-start(bf16[64,128]{1,0:T(8,128)(2,1)S(1)} %get-tuple-element.5), channel_id=1, source_target_pairs={{2,0},{4,2},{6,4},{8,6},{10,8},{12,10},{14,12},{16,14},{18,16},{20... | collective-permute-start | bytes 49160 | tf_op jit(solution)/shard_map/ppermute | solution.py:22
  51.0 0.0 copy-done.4
  51.0 0.4 copy.23
  51.4 0.6 reshape.80
  52.0 0.0 copy-done.5
  52.0 0.1 copy.28
  52.1 0.1 reshape.88
  52.2 0.0 copy-done.3
  52.3 1.1 convert_element_type.40
  53.3 1.4 copy.22
  54.7 1.4 copy.24
  56.1 8.9 %copy.25 = bf16[1,2048,128]{2,0,1:T(2,128)(2,1)} copy(bf16[1,2048,128]{2,1,0:T(8,128)(2,1)S(1)} %bitcast.45) | data formatting | bytes 1048576 | tf_op jit(solution)/shard_map/stack | solution.py:41
  65.0 49.4 %collective-permute-done = bf16[64,128]{1,0:T(8,128)(2,1)S(1)} collective-permute-done((bf16[64,128]{1,0:T(8,128)(2,1)S(1)}, bf16[64,128]{1,0:T(8,128)(2,1)S(1)}, u32[]{:S(2)}, u32[]{:S(2)}) %collective-permute-start) | collective-permute-done | bytes 16416 | tf_op jit(solution)/shard_map/ppermute | solution.py:19
  114.4 0.0 collective-permute-done.1
  114.5 24.0 %gather_fusion = bf16[8192,128]{1,0:T(8,128)(2,1)S(1)} fusion(bf16[2176,128]{1,0:T(8,128)(2,1)S(1)} %pad_maximum_fusion.1, s32[8192]{0:T(1024)S(1)} %broadcast_clamp_fusion.1), kind=kCustom, calls=%fused_computation | custom fusion | bytes 4227072 | tf_op jit(solution)/shard_map/gather | solution.py:38
  138.5 0.0 copy-start.2
  138.5 15.1 %fusion.2 = (bf16[2048,128]{1,0:T(8,128)(2,1)S(1)}, bf16[2048,128]{1,0:T(8,128)(2,1)S(1)}) fusion(bf16[2048,4,128]{2,1,0:T(4,128)(2,1)S(1)} %bitcast.44, f32[2048,128]{1,0:T(8,128)} %convert_element_type.40, f32[2048,4]{1,0:T(8,128)} %copy.22, f32[2048,4]{1,0:T(8,128)} %copy.24), kind=kLoop, calls=%fused_computation.9 | loop fusion | flops 5767168 | bytes 4259840 | tf_op jit(solution)/shard_map/reduce_sum | solution.py:39
  153.6 8.1 %copy.26 = bf16[1,2048,128]{2,0,1:T(2,128)(2,1)S(1)} copy(bf16[1,2048,128]{2,1,0:T(8,128)(2,1)S(1)} %bitcast.48) | data formatting | bytes 1048576 | tf_op jit(solution)/shard_map/convert_element_type | solution.py:39
  161.7 8.3 %copy.27 = bf16[1,2048,128]{2,0,1:T(2,128)(2,1)S(1)} copy(bf16[1,2048,128]{2,1,0:T(8,128)(2,1)S(1)} %bitcast.47) | data formatting | bytes 1048576 | tf_op jit(solution)/shard_map/convert_element_type | solution.py:40
  170.1 0.0 copy-done.2
  170.1 3.6 pad_maximum_fusion
  173.6 56.5 %gather_fusion.1 = bf16[8192,3,128]{2,1,0:T(4,128)(2,1)} fusion(bf16[3,2048,128]{2,0,1:T(4,128)(2,1)S(1)} %pad_maximum_fusion, s32[8192]{0:T(1024)S(1)} %broadcast_clamp_fusion), kind=kCustom, calls=%fused_computation.1 | custom fusion | bytes 12615680 | tf_op jit(solution)/shard_map/gather | solution.py:44
  230.1 8.0 %copy.29 = bf16[128,64,3,128]{3,1,2,0:T(8,128)(2,1)} copy(bf16[128,64,3,128]{3,2,1,0:T(4,128)(2,1)} %bitcast.41) | data formatting | bytes 12582912 | tf_op jit(solution)/shard_map/gather | solution.py:44
  238.1 7.8 %broadcast_in_dim.29 = bf16[256,192,128]{2,1,0:T(8,128)(2,1)} broadcast(bf16[]{:T(256)} %constant.16.clone.1), dimensions={} | broadcast | bytes 12582914 | tf_op jit(solution)/shard_map/broadcast_in_dim | solution.py:59
  245.9 21.5 %scatter_fusion = bf16[256,192,128]{2,1,0:T(8,128)(2,1)} fusion(bf16[256,192,128]{2,1,0:T(8,128)(2,1)} %broadcast_in_dim.29, s32[128]{0:T(128)S(1)} %fusion.13, bf16[128,192,128]{2,1,0:T(8,128)(2,1)} %bitcast.42), kind=kCustom, calls=%fused_computation.4 | custom fusion | bytes 18874880 | tf_op jit(solution)/shard_map/scatter | solution.py:59
  267.4 0.0 all-to-all-done.1
  267.4 9.6 %all-to-all-start.2 = ((bf16[256,192,128]{2,1,0:T(8,128)(2,1)}), bf16[256,192,128]{2,1,0:T(8,128)(2,1)}, u32[]{:S(2)}, u32[]{:S(2)}) async-start(bf16[256,192,128]{2,1,0:T(8,128)(2,1)} %scatter_fusion), calls=%async_computation.2 | async-start | bytes 25165824 | tf_op jit(solution)/shard_map/all_to_all | solution.py:62
  277.0 0.2 reshape.73
  277.2 16.0 %reshape.74 = bf16[256,192,32]{2,1,0:T(8,128)(2,1)} reshape(bf16[128,2,6144]{2,1,0:T(2,128)(2,1)} %all-to-all-done.1) | data formatting | bytes 6291456 | tf_op jit(solution)/shard_map/reshape | solution.py:29
  293.2 256.1 %all-to-all-done.2 = bf16[256,192,128]{2,1,0:T(8,128)(2,1)} async-done(((bf16[256,192,128]{2,1,0:T(8,128)(2,1)}), bf16[256,192,128]{2,1,0:T(8,128)(2,1)}, u32[]{:S(2)}, u32[]{:S(2)}) %all-to-all-start.2) | async-done | bytes 12582944 | tf_op jit(solution)/shard_map/all_to_all | solution.py:62
  549.3 12.1 %fusion.17 = f32[256,32,128]{2,1,0:T(8,128)} fusion(bf16[256,192,32]{2,1,0:T(8,128)(2,1)} %reshape.74, bf16[256,192,128]{2,1,0:T(8,128)(2,1)} %all-to-all-done.2), kind=kOutput, calls=%fused_computation.39 | convolution fusion | flops 402653184 | bytes 19922944 | tf_op jit(solution)/shard_map/dot_general | solution.py:30
  561.3 44.4 %scatter_custom_fusion.3 = f32[1024,128]{1,0:T(8,128)S(1)} fusion(s32[8192]{0:T(1024)S(1)} %bitcast.51, f32[8192,128]{1,0:T(8,128)} %bitcast.43, f32[]{:T(128)} %constant.11.clone.1), kind=kCustom, calls=%fused_computation.19 | custom fusion | flops 1048576 | bytes 524800 | tf_op jit(solution)/shard_map/scatter-add | solution.py:69
  605.8 0.2 copy.31
  606.0 0.7 convert_element_type.45
  606.7 0.0 copy-done
  606.7 28.9 %fusion.6 = f32[1,1024,32]{0,1,2:T(8,128)} fusion(f32[1024,4,32]{0,2,1:T(8,128)S(1)} %bitcast.46, f32[8]{0:T(128)S(1)} %copy-done, s32[]{:T(128)S(6)} %select_n.29), kind=kOutput, calls=%fused_computation.15 | convolution fusion | flops 1572864 | bytes 655396 | tf_op jit(solution)/shard_map/tlf,l->ft/dot_general | solution.py:76
  635.6 10.0 %copy.34 = f32[1,1024,32]{1,2,0:T(8,128)S(1)} copy(f32[1,1024,32]{0,1,2:T(8,128)} %fusion.6) | data formatting | bytes 262144 | tf_op jit(solution)/shard_map/tlf,l->ft/dot_general | solution.py:76
  645.5 7.5 %all-gather = f32[64,1024]{1,0:T(8,128)S(1)} all-gather(f32[32,1024]{1,0:T(8,128)S(1)} %bitcast.50), channel_id=2, replica_groups=mesh['src'=128,'lev'=2] {'lev'}, dimensions={0}, use_global_device_ids=true | all-gather | bytes 393216 | tf_op jit(solution)/shard_map/all_gather | solution.py:82
  653.0 0.7 reduce_sum.42
  (8 shorter events, 0.1 us)
Async XLA Ops:
  0.6 606.1 %copy-start = (f32[8]{0:T(128)S(1)}, f32[8]{0:T(128)}, u32[]{:S(2)}) copy-start(f32[8]{0:T(128)} %param.11) | copy-start | bytes 100
  5.4 27.3 %all-to-all-start = ((s32[128,2,32]{2,1,0:T(2,128)}), s32[128,2,32]{2,1,0:T(2,128)S(1)}, u32[]{:S(2)}, u32[]{:S(2)}) async-start(s32[128,2,32]{2,1,0:T(2,128)} %bitcast.3), calls=%async_computation | async-start | bytes 262144 | tf_op jit(solution)/shard_map/all_to_all | solution.py:58
  29.7 13.9 %copy-start.1 = (bf16[2048,128]{1,0:T(8,128)(2,1)S(1)}, bf16[2048,128]{1,0:T(8,128)(2,1)}, u32[]{:S(2)}) copy-start(bf16[2048,128]{1,0:T(8,128)(2,1)} %param.8) | copy-start | bytes 1572868
  29.7 21.3 %copy-start.4 = (s32[2048,4]{0,1:T(4,128)S(1)}, s32[2048,4]{0,1:T(4,128)}, u32[]{:S(2)}) copy-start(s32[2048,4]{0,1:T(4,128)} %param.10) | copy-start | bytes 98308
  29.7 22.3 %copy-start.5 = (s32[128,64]{0,1:T(8,128)S(1)}, s32[128,64]{0,1:T(8,128)}, u32[]{:S(2)}) copy-start(s32[128,64]{0,1:T(8,128)} %param.12) | copy-start | bytes 98308
  29.7 22.5 %copy-start.3 = (f32[2,4,2048]{2,1,0:T(4,128)S(1)}, f32[2,4,2048]{2,1,0:T(4,128)}, u32[]{:S(2)}) copy-start(f32[2,4,2048]{2,1,0:T(4,128)} %param.9) | copy-start | bytes 196612
  32.7 234.8 %all-to-all-start.1 = ((bf16[128,2,6144]{2,1,0:T(2,128)(2,1)}), bf16[128,2,6144]{2,1,0:T(2,128)(2,1)}, u32[]{:S(2)}, u32[]{:S(2)}) async-start(bf16[128,2,6144]{2,1,0:T(2,128)(2,1)} %all_to_all.17), calls=%async_computation.1 | async-start | bytes 6291456 | tf_op jit(solution)/shard_map/all_to_all | solution.py:63
  43.6 70.9 %collective-permute-start = (bf16[64,128]{1,0:T(8,128)(2,1)S(1)}, bf16[64,128]{1,0:T(8,128)(2,1)S(1)}, u32[]{:S(2)}, u32[]{:S(2)}) collective-permute-start(bf16[64,128]{1,0:T(8,128)(2,1)S(1)} %get-tuple-element.4), channel_id=1, source_target_pairs={{0,2},{2,4},{4,6},{6,8},{8,10},{10,12},{12,14},{14,16},{16,18},{18... | collective-permute-start | bytes 49160 | tf_op jit(solution)/shard_map/ppermute | solution.py:19
  44.2 70.3 %collective-permute-start.1 = (bf16[64,128]{1,0:T(8,128)(2,1)S(1)}, bf16[64,128]{1,0:T(8,128)(2,1)S(1)}, u32[]{:S(2)}, u32[]{:S(2)}) collective-permute-start(bf16[64,128]{1,0:T(8,128)(2,1)S(1)} %get-tuple-element.5), channel_id=1, source_target_pairs={{2,0},{4,2},{6,4},{8,6},{10,8},{12,10},{14,12},{16,14},{18,16},{20... | collective-permute-start | bytes 49160 | tf_op jit(solution)/shard_map/ppermute | solution.py:22
  138.5 31.5 %copy-start.2 = (bf16[1,2048,128]{2,0,1:T(2,128)(2,1)S(1)}, bf16[1,2048,128]{2,0,1:T(2,128)(2,1)}, u32[]{:S(2)}) copy-start(bf16[1,2048,128]{2,0,1:T(2,128)(2,1)} %copy.25) | copy-start | bytes 1572868
  267.4 281.9 %all-to-all-start.2 = ((bf16[256,192,128]{2,1,0:T(8,128)(2,1)}), bf16[256,192,128]{2,1,0:T(8,128)(2,1)}, u32[]{:S(2)}, u32[]{:S(2)}) async-start(bf16[256,192,128]{2,1,0:T(8,128)(2,1)} %scatter_fusion), calls=%async_computation.2 | async-start | bytes 25165824 | tf_op jit(solution)/shard_map/all_to_all | solution.py:62
